TPU v7x, 256 devices: a whole 4x4x8 slice. The times are simulated.
256 devices in a mesh: leaf: 64 (over x, z, core), rhs: 4 (over y).
Axes of the slice: x: 4, y: 4, z: 8, core: 2. Of those that a mesh axis runs over, the one named last changes fastest.
Arguments:
- fields: bfloat16 [131072, 1024], P('leaf', 'rhs'), may hold values from -6 to 6
- owner: int32 [131072, 1], P('leaf'), may hold values from 0 to 63; in each aligned block of 2048 rows (0 to 2047, 2048 to 4095, ...) at most 64 rows name the same one
- source_basis: bfloat16 [131072, 256], P('leaf'), may hold values from -0.125 to 0.125
- field_basis: bfloat16 [131072, 256], P('leaf'), may hold values from -0.375 to 0.375
- transfer: bfloat16 [64, 3, 256, 512], P('leaf', None, 'rhs'), may hold values from -0.25 to 0.25
- near_blocks: bfloat16 [512, 7, 256, 256], P('leaf'), may hold values from -0.25 to 0.25
- near_index: int32 [512, 7], P('leaf'), may hold values from 0 to 7
- near_count: int32 [512], P('leaf'), may hold values from 1 to 7
Outputs:
- scattered: bfloat16 [131072, 1024], P('leaf', 'rhs')
Inputs may be any that keep to these rules, and one draw needn't show every extreme that they name: In the rows of one group of 2048 rows at most 64 name one owner; in some group one owner is named by exactly 64. `near_index`: Row-block numbers counted within the same group of 8 row blocks.
All inputs are finite; a program needn't handle non-finite values.
Results may differ from a plain program's by a relative error of at most 0.006.
Values may be sent and summed in bfloat16 or wider, within the bound.
A program may use at most 128 MiB of HBM per device.

v0:
```python
import jax
import jax.numpy as jnp
from jax import lax
from jax.sharding import PartitionSpec as P


def swapped(value, axis, stride):
    return lax.ppermute(value, axis, [(i, i ^ 1 << stride) for i in range(lax.axis_size(axis))])


def slot_numbers(owners_of, n_leaf, capacity):
    onehot = (owners_of[:, None] == jnp.arange(n_leaf, dtype=jnp.int32)[None, :]).astype(jnp.int32)
    before = jnp.cumsum(onehot, axis=0) - onehot
    rank_in = jnp.sum(before * onehot, axis=1)
    return owners_of * capacity + rank_in


def on_device(
    fields, owner, source_basis, field_basis, transfer, near_blocks, near_index, near_count
):
    n_leaf = lax.axis_size("leaf")
    row_count, col_count = fields.shape
    basis_width = source_basis.shape[1]
    capacity = 2 * row_count // n_leaf
    slot_index = slot_numbers(owner[:, 0], n_leaf, capacity)
    block_rows = near_blocks.shape[2]
    block_count, near_slots = near_index.shape
    chosen = fields.reshape(block_count, block_rows, col_count)[near_index]
    keep_mask = jnp.arange(near_slots, dtype=jnp.int32)[None, :] < near_count[:, None]
    chosen = jnp.where(keep_mask[:, :, None, None], chosen, jnp.zeros((), jnp.bfloat16))
    near_term = jnp.einsum(
        "gjab,gjbn->gan", near_blocks, chosen, preferred_element_type=jnp.float32
    ).reshape(row_count, col_count)
    x_slots = jnp.zeros((n_leaf * capacity, col_count), jnp.bfloat16).at[slot_index].set(fields)
    v_slots = (
        jnp.zeros((n_leaf * capacity, basis_width), jnp.bfloat16).at[slot_index].set(source_basis)
    )
    u_slots = (
        jnp.zeros((n_leaf * capacity, basis_width), jnp.bfloat16).at[slot_index].set(field_basis)
    )
    x_three = x_slots.reshape(n_leaf, capacity, col_count)
    v_three = v_slots.reshape(n_leaf, capacity, basis_width)
    coefficients = lax.psum_scatter(
        jnp.einsum("bck,bcn->bkn", v_three, x_three, preferred_element_type=jnp.float32),
        "leaf",
        scatter_dimension=0,
        tiled=True,
    )[0].astype(jnp.bfloat16)
    for level_num in range(transfer.shape[1]):
        partner = swapped(coefficients, "leaf", level_num)
        stacked = jnp.concatenate([coefficients, partner], axis=0)

        def apply_rows(shard_piece, offset, stacked=stacked):
            return jnp.dot(shard_piece, stacked, preferred_element_type=jnp.float32)

        coefficients = apply_rows(
            lax.all_gather(transfer[0, level_num], "rhs", axis=0, tiled=True), jnp.int32(0)
        ).astype(jnp.bfloat16)
    u_three = u_slots.reshape(n_leaf, capacity, basis_width)
    far_slots = (
        jnp.einsum(
            "bck,bkn->bcn",
            u_three,
            lax.all_gather(coefficients[None], "leaf", axis=0, tiled=True),
            preferred_element_type=jnp.float32,
        )
        .astype(jnp.bfloat16)
        .reshape(n_leaf * capacity, col_count)
    )
    far_term = far_slots[slot_index]
    return (far_term.astype(jnp.float32) + near_term).astype(jnp.bfloat16)


def solution(mesh):
    in_specs = (
        P("leaf", "rhs"),
        P("leaf", None),
        P("leaf", None),
        P("leaf", None),
        P("leaf", None, "rhs", None),
        P("leaf", None, None, None),
        P("leaf", None),
        P("leaf"),
    )
    out_specs = P("leaf", "rhs")
    return jax.shard_map(
        on_device, mesh=mesh, in_specs=in_specs, out_specs=out_specs, check_vma=False
    )
```

profile of v0, /device:TPU:1, one launch (start us, length us, event | category | flops | bytes accessed | tf_op | source)
XLA Modules:
  0.0 411.4 jit_solution(9575077675460994863)
XLA Ops:
  6.5 0.8 fusion.17
  7.3 18.1 %reduce-window.6 = s32[64,16,128]{2,1,0:T(8,128)S(1)} reduce-window(s32[64,16,128]{2,1,0:T(8,128)S(1)} %fusion.17, s32[]{:T(128)} %constant.7.clone.1), window={size=1x1x128 pad=0_0x0_0x127_0}, to_apply=%region_0.0 | reduce-window | flops 16646144 | bytes 1048580 | tf_op jit(solution)/shard_map/reduce-window
  25.7 0.4 copy.14
  26.5 0.3 fusion.16
  26.8 10.4 %scatter_custom_fusion.1 = bf16[4096,256]{1,0:T(8,128)(2,1)S(1)} fusion(s32[2048]{0:T(1024)S(1)} %bitcast.75, bf16[2048,256]{1,0:T(8,128)(2,1)} %param.10, bf16[]{:T(256)} %constant.5.clone.1), kind=kCustom, calls=%fused_computation.20 | custom fusion | bytes 2097664 | tf_op jit(solution)/shard_map/scatter | solution.py:36
  37.2 10.9 %scatter_custom_fusion.2 = bf16[4096,256]{1,0:T(8,128)(2,1)} fusion(s32[2048]{0:T(1024)S(1)} %bitcast.76, bf16[2048,256]{1,0:T(8,128)(2,1)S(1)} %copy-done, bf16[]{:T(256)} %constant.5.clone.1), kind=kCustom, calls=%fused_computation.18 | custom fusion | bytes 2097154 | tf_op jit(solution)/shard_map/scatter | solution.py:34
  48.1 9.7 %fusion.35 = f32[64,256,256]{2,1,0:T(8,128)} fusion(bf16[64,64,256]{2,1,0:T(8,128)(2,1)S(1)} %bitcast.66, bf16[64,64,256]{2,1,0:T(8,128)(2,1)} %bitcast.67), kind=kOutput, calls=%fused_computation.55 | convolution fusion | flops 536870912 | bytes 20971520 | tf_op jit(solution)/shard_map/bck,bcn->bkn/dot_general | solution.py:44
  57.9 189.7 %reduce-scatter.2.cloned.1.call-done = f32[1,256,256]{2,1,0:T(8,128)} async-done(((f32[64,256,256]{2,1,0:T(8,128)}), f32[1,256,256]{2,1,0:T(8,128)}) %reduce-scatter.2.cloned.1.call-update) | async-done | bytes 262160 | tf_op jit(solution)/shard_map/reduce_scatter | solution.py:43
  247.5 1.0 convert_bitcast_fusion
  248.5 4.7 %collective-permute-start = (bf16[256,256]{1,0:T(8,128)(2,1)S(1)}, bf16[256,256]{1,0:T(8,128)(2,1)S(1)}, u32[]{:S(2)}, u32[]{:S(2)}) collective-permute-start(bf16[256,256]{1,0:T(8,128)(2,1)S(1)} %convert_bitcast_fusion), channel_id=1, source_target_pairs={{0,4},{4,0},{8,12},{12,8},{16,20},{20,16},{24,28},{28,24},{32,36},... | collective-permute-start | bytes 393224 | tf_op jit(solution)/shard_map/ppermute | solution.py:8
  253.3 10.1 %all-gather = bf16[1,1,256,512]{3,2,1,0:T(8,128)(2,1)S(1)} all-gather(bf16[1,1,64,512]{3,2,1,0:T(8,128)(2,1)S(1)} %get-tuple-element.6), channel_id=2, replica_groups=mesh['leaf'=64,'rhs'=4] {'rhs'}, dimensions={2}, use_global_device_ids=true | all-gather | bytes 327680 | tf_op jit(solution)/shard_map/all_gather | solution.py:57
  263.6 0.4 collective-permute-start.1
  264.0 9.4 %all-gather.1 = bf16[1,1,256,512]{3,2,1,0:T(8,128)(2,1)S(1)} all-gather(bf16[1,1,64,512]{3,2,1,0:T(8,128)(2,1)S(1)} %get-tuple-element.7), channel_id=3, replica_groups=mesh['leaf'=64,'rhs'=4] {'rhs'}, dimensions={2}, use_global_device_ids=true | all-gather | bytes 327680 | tf_op jit(solution)/shard_map/all_gather | solution.py:57
  273.6 1.9 collective-permute-start.2
  275.6 9.5 %all-gather.2 = bf16[1,1,256,512]{3,2,1,0:T(8,128)(2,1)S(1)} all-gather(bf16[1,1,64,512]{3,2,1,0:T(8,128)(2,1)S(1)} %get-tuple-element.5), channel_id=4, replica_groups=mesh['leaf'=64,'rhs'=4] {'rhs'}, dimensions={2}, use_global_device_ids=true | all-gather | bytes 327680 | tf_op jit(solution)/shard_map/all_gather | solution.py:57
  285.1 0.9 fusion.5
  286.0 11.2 %scatter_custom_fusion = bf16[4096,256]{1,0:T(8,128)(2,1)} fusion(s32[2048]{0:T(1024)S(1)} %bitcast.77, bf16[2048,256]{1,0:T(8,128)(2,1)} %param.11, bf16[]{:T(256)} %constant.5.clone.1), kind=kCustom, calls=%fused_computation.22 | custom fusion | bytes 2097664 | tf_op jit(solution)/shard_map/scatter | solution.py:39
  297.4 5.3 %gather_fusion.1 = bf16[56,256,256]{2,1,0:T(8,128)(2,1)} fusion(bf16[8,256,256]{2,1,0:T(8,128)(2,1)S(1)} %bitcast.64, s32[1024]{0:T(1024)S(1)} %pad_clamp_fusion), kind=kCustom, calls=%fused_computation.1 | custom fusion | bytes 14680288 | tf_op jit(solution)/shard_map/gather | solution.py:28
  302.8 8.8 %fusion = f32[8,256,256,1]{1,2,3,0:T(8,128)} fusion(bf16[8,7,256,256]{3,2,1,0:T(8,128)(2,1)} %param.13, bf16[8,7,256,256]{3,2,1,0:T(8,128)(2,1)} %bitcast.68, pred[8,7]{1,0:T(8,128)(4,1)S(1)} %iota_compare_fusion.2), kind=kOutput, calls=%fused_computation.5 | convolution fusion | flops 1882718208 | bytes 16777272 | tf_op jit(solution)/shard_map/gjab,gjbn->gan/dot_general | solution.py:31
  311.5 65.2 %all-gather.6.cloned.1.call-done = bf16[16384,256]{0,1:T(8,128)(2,1)} async-done(((bf16[256,256]{0,1:T(8,128)(2,1)}), bf16[16384,256]{0,1:T(8,128)(2,1)}) %all-gather.6.cloned.1.call-update) | async-done | bytes 8388624 | tf_op jit(solution)/shard_map/all_gather | solution.py:64
  376.8 11.9 %copy.15 = bf16[16384,256]{1,0:T(8,128)(2,1)} copy(bf16[16384,256]{0,1:T(8,128)(2,1)} %all-gather.6.cloned.1.call-done) | data formatting | bytes 16777216 | tf_op jit(solution)/shard_map/all_gather | solution.py:64
  388.6 5.6 %convolution_convert_fusion = bf16[64,64,256]{2,1,0:T(8,128)(2,1)S(1)} fusion(bf16[64,64,256]{2,1,0:T(8,128)(2,1)} %bitcast.65, bf16[64,256,256]{2,1,0:T(8,128)(2,1)} %bitcast.63), kind=kOutput, calls=%fused_computation.11 | convolution fusion | flops 537919488 | bytes 12582912 | tf_op jit(solution)/shard_map/bck,bkn->bcn/dot_general | solution.py:61
  394.2 7.5 %gather_fusion = bf16[2048,256]{1,0:T(8,128)(2,1)S(1)} fusion(bf16[4096,256]{1,0:T(8,128)(2,1)S(1)} %bitcast.62, s32[2048]{0:T(1024)S(1)} %broadcast_clamp_fusion), kind=kCustom, calls=%fused_computation | custom fusion | bytes 2105344 | tf_op jit(solution)/shard_map/gather | solution.py:70
  401.7 2.8 fusion.4
  (29 shorter events, 1.4 us)
Async XLA Ops:
  6.5 241.0 %reduce-scatter.2.cloned.1.call-start = ((), (), s32[]{:S(2)}) async-start(), calls=%async_computation.1 | async-start | bytes 17039360 | tf_op jit(solution)/shard_map/reduce_scatter | solution.py:43
  6.5 20.0 %copy-start.2 = (s32[2048,1]{0,1:T(1,128)S(1)}, s32[2048,1]{0,1:T(1,128)}, u32[]{:S(2)}) copy-start(s32[2048,1]{0,1:T(1,128)} %param.9) | copy-start | bytes 24580
  25.7 11.5 %copy-start = (bf16[2048,256]{1,0:T(8,128)(2,1)S(1)}, bf16[2048,256]{1,0:T(8,128)(2,1)}, u32[]{:S(2)}) copy-start(bf16[2048,256]{1,0:T(8,128)(2,1)} %param.8) | copy-start | bytes 3145732
  57.8 195.4 %copy-start.1 = (bf16[1,3,64,512]{3,2,1,0:T(8,128)(2,1)S(1)}, bf16[1,3,64,512]{3,2,1,0:T(8,128)(2,1)}, u32[]{:S(2)}) copy-start(bf16[1,3,64,512]{3,2,1,0:T(8,128)(2,1)} %param.12) | copy-start | bytes 589828
  57.8 318.9 %all-gather.6.cloned.1.call-start = ((), (), s32[]{:S(2)}) async-start(), calls=%async_computation.2 | async-start | bytes 8519680 | tf_op jit(solution)/shard_map/all_gather | solution.py:64
  248.5 14.9 %collective-permute-start = (bf16[256,256]{1,0:T(8,128)(2,1)S(1)}, bf16[256,256]{1,0:T(8,128)(2,1)S(1)}, u32[]{:S(2)}, u32[]{:S(2)}) collective-permute-start(bf16[256,256]{1,0:T(8,128)(2,1)S(1)} %convert_bitcast_fusion), channel_id=1, source_target_pairs={{0,4},{4,0},{8,12},{12,8},{16,20},{20,16},{24,28},{28,24},{32,36},... | collective-permute-start | bytes 393224 | tf_op jit(solution)/shard_map/ppermute | solution.py:8
  263.6 9.8 %collective-permute-start.1 = (bf16[256,256]{1,0:T(8,128)(2,1)S(1)}, bf16[256,256]{1,0:T(8,128)(2,1)S(1)}, u32[]{:S(2)}, u32[]{:S(2)}) collective-permute-start(bf16[256,256]{1,0:T(8,128)(2,1)S(1)} %fusion.6), channel_id=1, source_target_pairs={{0,8},{4,12},{8,0},{12,4},{16,24},{20,28},{24,16},{28,20},{32,40},... | collective-permute-start | bytes 393224 | tf_op jit(solution)/shard_map/ppermute | solution.py:8
  273.4 23.9 %copy-start.3 = (s32[8,7]{1,0:T(8,128)S(1)}, s32[8,7]{1,0:T(8,128)}, u32[]{:S(2)}) copy-start(s32[8,7]{1,0:T(8,128)} %param.14) | copy-start | bytes 676
  273.6 11.4 %collective-permute-start.2 = (bf16[256,256]{1,0:T(8,128)(2,1)S(1)}, bf16[256,256]{1,0:T(8,128)(2,1)S(1)}, u32[]{:S(2)}, u32[]{:S(2)}) collective-permute-start(bf16[256,256]{1,0:T(8,128)(2,1)S(1)} %fusion.7), channel_id=1, source_target_pairs={{0,16},{4,20},{8,24},{12,28},{16,0},{20,4},{24,8},{28,12},{32,48},... | collective-permute-start | bytes 393224 | tf_op jit(solution)/shard_map/ppermute | solution.py:8
  297.4 5.3 %copy-start.4 = (s32[8]{0:T(128)S(1)}, s32[8]{0:T(128)}, u32[]{:S(2)}) copy-start(s32[8]{0:T(128)} %param.15) | copy-start | bytes 100
Sparse Core Ops, SparseCore 0:
  58.0 189.5 reduce-scatter.1
  286.2 90.5 all-gather.5
where the time goes:
time: 412 us; the launch traced here: 411 us
  waiting for transfers between devices  255 us (62%)
  local copies, waits for them, and re-layouts  57.9 us (14%)
  blocking collectives  28.9 us (7%)
  matrix products  25.4 us (6%)
  other arithmetic  23.5 us (6%)
  between operations  13.5 us (3%)
  starting transfers between devices  7.18 us (2%)
    reduce_scatter x1, waiting for transfers between devices, on_device(): lax.psum_scatter(jnp.einsum('bck,bcn->bkn', v_three, x_three, preferred_e...  190 us
    all_gather x1, waiting for transfers between devices, on_device(): lax.all_gather(coefficients[None], 'leaf', axis=0, tiled=True)  65.2 us
    all_gather x3, blocking collectives, on_device(): lax.all_gather(transfer[0, level_num], 'rhs', axis=0, tiled=True)  28.9 us
    scatter x2, local copies, waits for them, and re-layouts, on_device(): jnp.zeros((n_leaf * capacity, basis_width), jnp.bfloat16).at[slot_index]  21.6 us
    another operation x3, other arithmetic  18.5 us
    all_gather x1, local copies, waits for them, and re-layouts, on_device(): lax.all_gather(coefficients[None], 'leaf', axis=0, tiled=True)  11.9 us
    scatter x1, local copies, waits for them, and re-layouts, on_device(): jnp.zeros((n_leaf * capacity, col_count), jnp.bfloat16).at[slot_index]  10.9 us
    dot_general x1, matrix products, on_device(): jnp.einsum('bck,bcn->bkn', v_three, x_three, preferred_element_type=jnp.f...  9.68 us
  transfers between devices with their start and end apart: 5, of which 2 were waited for; matrix products, arithmetic and copies ran while one was open for 6% of the time, Pallas kernels for 0%

commit v1 on v0

v1 whole, which is shorter than its diff:
```python
import jax
import jax.numpy as jnp
from jax import lax
from jax.experimental import pallas as pl
from jax.experimental.pallas import tpu as pltpu
from jax.sharding import PartitionSpec as P

MESH = pl.DeviceIdType.MESH
F32 = jnp.float32
BF16 = jnp.bfloat16
CAP = 64
NX, NZ, NC, NY = 4, 8, 2, 4
NB = NX * NZ * NC


def slot_kernel(owner_ref, slot_ref):
    rows = owner_ref.shape[1]
    step = 256
    below = lax.broadcasted_iota(jnp.int32, (step, step), 0)
    above = lax.broadcasted_iota(jnp.int32, (step, step), 1)
    tri = (below < above).astype(F32).astype(BF16)
    carry = jnp.zeros((NB, 1), F32)
    names = lax.broadcasted_iota(jnp.int32, (NB, step), 0)
    for i in range(rows // step):
        own = owner_ref[:, i * step : (i + 1) * step]
        hot = (names == own).astype(F32)
        before = jnp.dot(hot.astype(BF16), tri, preferred_element_type=F32) + carry
        rank = jnp.sum(before * hot, axis=0, keepdims=True)
        slot_ref[:, i * step : (i + 1) * step] = own * CAP + rank.astype(jnp.int32)
        carry = carry + jnp.sum(hot, axis=1, keepdims=True)


def slots_of(owner_row):
    return pl.pallas_call(
        slot_kernel,
        out_shape=jax.ShapeDtypeStruct(owner_row.shape, jnp.int32),
        in_specs=[pl.BlockSpec(memory_space=pltpu.VMEM)],
        out_specs=pl.BlockSpec(memory_space=pltpu.VMEM),
    )(owner_row)


def leaf_id(x, z, c):
    return x * (NZ * NC) + z * NC + c


def far_kernel(
    slot_ref, x_ref, v_ref, u_ref, t_ref, far_ref,
    sx, rx, us, ring, lvl, part, tg, cb,
    xs_sem, xr_sem, rs_sem, rr_sem, bs_sem, br_sem, ts_sem, tr_sem,
    zs_sem, zr_sem, hs_sem, hr_sem, fs_sem, fr_sem, cs_sem, cr_sem,
):
    leaf = lax.axis_index("leaf")
    y = lax.axis_index("rhs")
    x = leaf // (NZ * NC)
    z = (leaf // NC) % NZ
    c = leaf % NC
    d = 1 - 2 * c

    def dev(xx, zz, cc):
        return {"leaf": leaf_id(xx % NX, zz % NZ, cc), "rhs": y}

    def remote(src, dst, ssem, rsem, who):
        return pltpu.make_async_remote_copy(
            src_ref=src, dst_ref=dst, send_sem=ssem, recv_sem=rsem,
            device_id=who, device_id_type=MESH,
        )

    barrier = pltpu.get_barrier_semaphore()
    peers = [dev(x + dx, z, (c + dc) % NC) for dx in range(NX) for dc in range(NC) if dx or dc]
    z4 = (z // 4) * 4
    z2 = z4 + (z - z4 + 2) % 4
    z1 = (z // 2) * 2 + (1 - z % 2)
    peers += [dev(x, z + 1, c), dev(x, z + NZ - 1, c), dev(x, z2, c)]
    peers += [{"leaf": leaf, "rhs": (y + k) % NY} for k in range(1, NY)]
    for who in peers:
        pl.semaphore_signal(barrier, inc=1, device_id=who, device_id_type=MESH)
    pl.semaphore_wait(barrier, len(peers))

    tcopies = [
        remote(t_ref, tg.at[:, y], ts_sem.at[k - 1], tr_sem.at[k - 1], {"leaf": leaf, "rhs": (y + k) % NY})
        for k in range(1, NY)
    ]
    for cp in tcopies:
        cp.start()
    tg[:, y] = t_ref[...]

    ranks = lax.broadcasted_iota(jnp.int32, (CAP, 1), 0)

    def permute(i, carry):
        slots = slot_ref[...]
        hots = []
        for k in range(NX * NC):
            xx, cc = (x + k // NC) % NX, (c + k % NC) % NC
            zz = (z + NZ - (1 - 2 * cc) * (i + 1)) % NZ
            want = ranks + leaf_id(xx, zz, cc) * CAP
            hots.append((slots == want).astype(F32).astype(BF16))
        hot = jnp.concatenate(hots, axis=0)
        xp = jnp.dot(hot, x_ref[...], preferred_element_type=F32).astype(BF16)
        vp = jnp.dot(hot, v_ref[...], preferred_element_type=F32).astype(BF16)
        rx[i, 0, :, 0:256] = xp[0:CAP]
        rx[i, 0, :, 256:512] = vp[0:CAP]
        sx[i, :, :, 0:256] = xp[CAP:].reshape(NX * NC - 1, CAP, 256)
        sx[i, :, :, 256:512] = vp[CAP:].reshape(NX * NC - 1, CAP, 256)
        for k in range(1, NX * NC):
            remote(
                sx.at[i, k - 1], rx.at[i, k], xs_sem.at[i], xr_sem.at[i],
                dev(x + k // NC, z, (c + k % NC) % NC),
            ).start()
        return carry

    lax.fori_loop(0, NZ, permute, 0)

    def permute_u(i, carry):
        want = lax.broadcasted_iota(jnp.int32, (8 * CAP, 1), 0) + i * (8 * CAP)
        hot = (slot_ref[...] == want).astype(F32).astype(BF16)
        up = jnp.dot(hot, u_ref[...], preferred_element_type=F32).astype(BF16)
        us[pl.ds(i * 8, 8)] = up.reshape(8, CAP, 256)
        return carry

    lax.fori_loop(0, NB // 8, permute_u, 0)

    def product(i):
        pltpu.make_async_copy(rx.at[i, pl.ds(1, 7)], rx.at[i, pl.ds(1, 7)], xr_sem.at[i]).wait()
        vs = rx[i, :, :, 256:512].reshape(NX * NC * CAP, 256)
        xs = rx[i, :, :, 0:256].reshape(NX * NC * CAP, 256)
        return lax.dot_general(vs, xs, (((0,), (0,)), ((), ())), preferred_element_type=F32)

    nxt = dev(x, z + NZ + d, c)

    def ring_copy(s, q):
        return remote(ring.at[s, q], ring.at[s + 1, q], rs_sem.at[s, q], rr_sem.at[s, q], nxt)

    first = product(0)
    for q in range(2):
        ring[0, q] = first[128 * q : 128 * q + 128]
        ring_copy(0, q).start()

    def ring_step(s, carry):
        p = product(s)
        for q in range(2):
            ring_copy(s - 1, q).wait_recv()
            ring[s, q] = ring[s, q] + p[128 * q : 128 * q + 128]
            ring_copy(s, q).start()
        return carry

    lax.fori_loop(1, NZ - 1, ring_step, 0)
    last = product(NZ - 1)
    for q in range(2):
        ring_copy(NZ - 2, q).wait_recv()
        lvl[0, 128 * q : 128 * q + 128, :] = (ring[NZ - 1, q] + last[128 * q : 128 * q + 128]).astype(BF16)

    for cp in tcopies:
        cp.wait_recv()

    mates = [dev(x, z, 1 - c), dev(x, z1, c), dev(x, z2, c)]
    bcopies = []
    for l in range(3):
        cp = remote(lvl.at[l], part.at[l], bs_sem.at[l], br_sem.at[l], mates[l])
        cp.start()
        bcopies.append(cp)
        t = tg[l].reshape(256, 512)
        acc = jnp.dot(t[:, 0:256], lvl[l], preferred_element_type=F32)
        cp.wait_recv()
        acc = acc + jnp.dot(t[:, 256:512], part[l], preferred_element_type=F32)
        if l < 2:
            lvl[l + 1] = acc.astype(BF16)
        else:
            cb[leaf] = acc.astype(BF16)

    waits = []

    def go(cp):
        cp.start()
        waits.append(cp)

    def zsend(sign, j):
        b = leaf_id(x, (z + 2 * NZ - sign * d * (j - 1)) % NZ, c)
        k = j - 1 if sign == 1 else 3 + j
        return remote(cb.at[b], cb.at[b], zs_sem.at[k], zr_sem.at[k], dev(x, z + NZ + sign * d, c))

    order = [0, 1, -1, 2, -2, 3, -3, 4]

    def zpos(n):
        return (z + 2 * NZ - d * order[n]) % NZ

    def have(b, n):
        go(remote(cb.at[b], cb.at[b], cs_sem.at[n], cr_sem.at[n], dev(x, z, 1 - c)))

    def xsend(n, way):
        b = leaf_id(x, zpos(n), c)
        return remote(cb.at[b], cb.at[b], hs_sem.at[n, way], hr_sem.at[n, way], dev(x + (1 if way == 0 else NX - 1), z, c))

    def fsend(n, way):
        b = leaf_id((x + (NX - 1 if way == 0 else 1)) % NX, zpos(n), c)
        half = pl.ds(128 * way, 128)
        return remote(
            cb.at[b, half], cb.at[b, half], fs_sem.at[n, way], fr_sem.at[n, way],
            dev(x + (1 if way == 0 else NX - 1), z, c),
        )

    def xdone(n):
        for way in range(2):
            xsend(n, way).wait_recv()
            go(fsend(n, way))
            have(leaf_id((x + (NX - 1 if way == 0 else 1)) % NX, zpos(n), c), 8 + 2 * n + way)

    def xtwo(n):
        for way in range(2):
            fsend(n, way).wait_recv()
        have(leaf_id((x + 2) % NX, zpos(n), c), 24 + n)

    go(zsend(1, 1))
    go(zsend(-1, 1))
    for n in range(8):
        if n > 0:
            sign, j = (1, order[n]) if order[n] > 0 else (-1, -order[n])
            zsend(sign, j).wait_recv()
            if (sign == 1 and j < 4) or (sign == -1 and j < 3):
                go(zsend(sign, j + 1))
        go(xsend(n, 0))
        go(xsend(n, 1))
        have(leaf_id(x, zpos(n), c), n)
        if n > 1:
            xdone(n - 2)
        if n > 3:
            xtwo(n - 4)
    xdone(6)
    xdone(7)
    for n in range(4, 8):
        xtwo(n)
    for n in range(32):
        remote(cb.at[leaf], cb.at[leaf], cs_sem.at[n], cr_sem.at[n], dev(x, z, 1 - c)).wait_recv()

    def far_one(b, carry):
        far_ref[b] = jnp.dot(us[b], cb[b], preferred_element_type=F32).astype(BF16)
        return carry

    lax.fori_loop(0, NB, far_one, 0)

    for cp in waits:
        cp.wait_send()
    for cp in bcopies:
        cp.wait_send()
    for cp in tcopies:
        cp.wait_send()
    for i in range(NZ):
        pltpu.make_async_copy(sx.at[i], sx.at[i], xs_sem.at[i]).wait()
    for s in range(NZ - 1):
        for q in range(2):
            ring_copy(s, q).wait_send()


def far_slots(slot_row, fields, source_basis, field_basis, transfer):
    vmem = pl.BlockSpec(memory_space=pltpu.VMEM)
    dma = pltpu.SemaphoreType.DMA
    return pl.pallas_call(
        far_kernel,
        out_shape=jax.ShapeDtypeStruct((NB, CAP, 256), BF16),
        in_specs=[vmem] * 5,
        out_specs=vmem,
        scratch_shapes=[
            pltpu.VMEM((NZ, 7, CAP, 512), BF16),
            pltpu.VMEM((NZ, 8, CAP, 512), BF16),
            pltpu.VMEM((NB, CAP, 256), BF16),
            pltpu.VMEM((NZ, 2, 128, 256), F32),
            pltpu.VMEM((3, 256, 256), BF16),
            pltpu.VMEM((3, 256, 256), BF16),
            pltpu.VMEM((3, NY, 64, 512), BF16),
            pltpu.VMEM((NB, 256, 256), BF16),
            dma((NZ,)), dma((NZ,)),
            dma((NZ, 2)), dma((NZ, 2)),
            dma((3,)), dma((3,)),
            dma((3,)), dma((3,)),
            dma((8,)), dma((8,)),
            dma((8, 2)), dma((8, 2)),
            dma((8, 2)), dma((8, 2)),
            dma((32,)), dma((32,)),
        ],
        compiler_params=pltpu.CompilerParams(
            collective_id=0, has_side_effects=True, vmem_limit_bytes=60 * 1024 * 1024
        ),
    )(slot_row, fields, source_basis, field_basis, transfer)


def out_kernel(index_ref, count_ref, blocks_ref, fields_ref, slot_ref, far_ref, out_ref):
    g = pl.program_id(0)
    slots = slot_ref[...]
    acc = None
    for i in range(4):
        want = lax.broadcasted_iota(jnp.int32, (1, 1024), 1) + i * 1024
        hot = (slots == want).astype(F32).astype(BF16)
        piece = jnp.dot(hot, far_ref[i * 1024 : (i + 1) * 1024, :], preferred_element_type=F32)
        acc = piece if acc is None else acc + piece

    def near(j, total):
        src = pl.multiple_of(index_ref[g * 7 + j] * 256, 256)
        return total + jnp.dot(blocks_ref[0, j], fields_ref[pl.ds(src, 256), :], preferred_element_type=F32)

    acc = acc + lax.fori_loop(0, count_ref[g], near, jnp.zeros((256, 256), F32))
    out_ref[...] = acc.astype(BF16)


def combine(near_index, near_count, near_blocks, fields, slot_col, far):
    return pl.pallas_call(
        out_kernel,
        out_shape=jax.ShapeDtypeStruct((2048, 256), BF16),
        grid_spec=pltpu.PrefetchScalarGridSpec(
            num_scalar_prefetch=2,
            grid=(8,),
            in_specs=[
                pl.BlockSpec((1, 7, 256, 256), lambda g, a, b: (g, 0, 0, 0)),
                pl.BlockSpec((2048, 256), lambda g, a, b: (0, 0)),
                pl.BlockSpec((256, 1), lambda g, a, b: (g, 0)),
                pl.BlockSpec((4096, 256), lambda g, a, b: (0, 0)),
            ],
            out_specs=pl.BlockSpec((256, 256), lambda g, a, b: (g, 0)),
        ),
    )(near_index.reshape(-1), near_count, near_blocks, fields, slot_col, far)


def on_device(
    fields, owner, source_basis, field_basis, transfer, near_blocks, near_index, near_count
):
    slot_row = slots_of(owner.reshape(1, -1))
    far = far_slots(slot_row, fields, source_basis, field_basis, transfer[0])
    return combine(
        near_index, near_count, near_blocks, fields, slot_row.reshape(-1, 1), far.reshape(NB * CAP, 256)
    )


def solution(mesh):
    in_specs = (
        P("leaf", "rhs"),
        P("leaf", None),
        P("leaf", None),
        P("leaf", None),
        P("leaf", None, "rhs", None),
        P("leaf", None, None, None),
        P("leaf", None),
        P("leaf"),
    )
    return jax.shard_map(
        on_device, mesh=mesh, in_specs=in_specs, out_specs=P("leaf", "rhs"), check_vma=False
    )
```

time: 412 us -> 147 us (0.36)
  waiting for transfers between devices: 255 us -> 0 us
  Pallas kernels: 0 us -> 143 us
  local copies, waits for them, and re-layouts: 57.9 us -> 3.29 us
  blocking collectives: 28.9 us -> 0 us
  matrix products: 25.4 us -> 0 us
  other arithmetic: 23.5 us -> 0 us
  between operations: 13.5 us -> 0.01 us
  starting transfers between devices: 7.18 us -> 0 us
    reduce_scatter x1 -> x0, waiting for transfers between devices: 190 us -> none  [on_device(): lax.psum_scatter(jnp.einsum('bck,bcn->bkn', v_three, x_three, preferred_e...]
    pallas_call x0 -> x3, Pallas kernels: none -> 143 us  [the longest x1 124 us: far_slots(): pl.pallas_call(far_kernel, out_shape=jax.ShapeDtypeStruct((NB, CAP, 256),...]
    all_gather x1 -> x0, waiting for transfers between devices: 65.2 us -> none  [on_device(): lax.all_gather(coefficients[None], 'leaf', axis=0, tiled=True)]
    scatter x3 -> x0, local copies, waits for them, and re-layouts: 32.5 us -> none  [the longest x2 21.6 us: on_device(): jnp.zeros((n_leaf * capacity, basis_width), jnp.bfloat16).at[slot_index]]
    all_gather x3 -> x0, blocking collectives: 28.9 us -> none  [on_device(): lax.all_gather(transfer[0, level_num], 'rhs', axis=0, tiled=True)]
    dot_general x6 -> x0, matrix products: 25.4 us -> none  [the longest x1 9.68 us: on_device(): jnp.einsum('bck,bcn->bkn', v_three, x_three, preferred_element_type=jnp.f...]
    another operation x3 -> x0, other arithmetic: 18.5 us -> none
    gather x2 -> x0, local copies, waits for them, and re-layouts: 12.8 us -> none  [the longest x1 7.5 us: on_device(): far_term = far_slots[slot_index]]
  transfers between devices with their start and end apart: 5 -> 0, of which waited for: 2 -> 0; matrix products, arithmetic and copies ran while one was open for 6% -> 0% of each run, Pallas kernels for 0% -> 0%
where the time goes in v1:
time: 147 us; the launch traced here: 146 us
  Pallas kernels  143 us (97%)
  local copies, waits for them, and re-layouts  3.29 us (2%)
    pallas_call x1, Pallas kernels, far_slots(): pl.pallas_call(far_kernel, out_shape=jax.ShapeDtypeStruct((NB, CAP, 256),...  124 us
    pallas_call x1, Pallas kernels, combine(): pl.pallas_call(out_kernel, out_shape=jax.ShapeDtypeStruct((2048, 256), BF...  17.2 us

profile of v1, /device:TPU:1, one launch (start us, length us, event | category | flops | bytes accessed | tf_op | source)
XLA Modules:
  0.0 146.2 jit_solution(1787104771612437424)
XLA Ops:
  0.0 1.2 reshape.12.index_ref
  1.2 1.6 %shard_map.82.slot_ref = s32[1,2048]{1,0:T(1,128)} custom-call(s32[1,2048]{1,0:T(1,128)} %bitcast.7), custom_call_target="tpu_custom_call" | custom-call | tf_op jit(solution)/shard_map/pallas_call | solution.py:34
  2.9 2.0 %copy.9.slot_ref = s32[2048,1]{1,0:T(8,128)} copy(s32[2048,1]{0,1:T(1,128)} %bitcast.6) | data formatting | bytes 16384 | tf_op jit(solution)/shard_map/reshape | solution.py:327
  4.9 124.1 %shard_map.83 = bf16[64,64,256]{2,1,0:T(8,128)(2,1)} custom-call(s32[1,2048]{1,0:T(1,128)} %shard_map.82.slot_ref, bf16[2048,256]{1,0:T(8,128)(2,1)} %fields_ref.1, bf16[2048,256]{1,0:T(8,128)(2,1)} %v_ref.1, bf16[2048,256]{1,0:T(8,128)(2,1)} %u_ref.1, bf16[3,64,512]{2,1,0:T(8,128)(2,1)} %bitcast.5), custom_call_target="tpu_custom_call" | custom-call | tf_op jit(solution)/shard_map/pallas_call | solution.py:256
  129.1 17.2 %shard_map.84 = bf16[2048,256]{1,0:T(8,128)(2,1)} custom-call(s32[56]{0:T(128)} %reshape.12.index_ref, s32[8]{0:T(128)} %count_ref.1, bf16[8,7,256,256]{3,2,1,0:T(8,128)(2,1)} %blocks_ref.1, bf16[2048,256]{1,0:T(8,128)(2,1)} %fields_ref.1, s32[2048,1]{1,0:T(8,128)} %copy.9.slot_ref, bf16[4096,256]{1,0:T(8,128)(2,1)} %bitcast.4), custom_call_target="tpu_custom_call" | custom-call | tf_op jit(solution)/shard_map/pallas_call | solution.py:304

commit v2 on v0

v2 whole, which is shorter than its diff:
```python
import jax
import jax.numpy as jnp
from jax import lax
from jax.experimental import pallas as pl
from jax.experimental.pallas import tpu as pltpu
from jax.sharding import PartitionSpec as P

MESH = pl.DeviceIdType.MESH
F32 = jnp.float32
BF16 = jnp.bfloat16
CAP = 64
NX, NZ, NC, NY = 4, 8, 2, 4
NB = NX * NZ * NC
NG = NX * NC
Q = CAP // NY
ROWS = 2048
HALF = 128
ES = [0, 1, -1, 2, -2, 3, -3, 4]
DIST = [0, 1, 1, 2]
SHIFT = [0, NX - 1, 1, 2]
ROUNDS = [[(e, f) for e in ES for f in range(4) if abs(e) + DIST[f] == r] for r in range(7)]
UNITS = [u for r in ROUNDS for u in r]
FILL = [[[0], []], [[1, 2], []], [[3, 4, 5, 6], [7]]]


def leaf_id(x, z, c):
    return x * (NZ * NC) + z * NC + c


def whole_kernel(
    owner_ref, index_ref, count_ref, x_hbm, v_hbm, u_hbm, t_hbm, n_hbm, out_ref,
    xb, vb, ub, nb, slot, scol, sx, sv, rx, rv, us, ring, lvl, part, tg, cb, acc,
    in_sem, n_sem,
    xs_sem, xr_sem, vs_sem, vr_sem, ys_sem, yr_sem, rs_sem, rr_sem, bs_sem, br_sem, ts_sem, tr_sem,
    zs_sem, zr_sem, hs_sem, hr_sem, fs_sem, fr_sem, cs_sem, cr_sem,
):
    leaf = lax.axis_index("leaf")
    y = lax.axis_index("rhs")
    x = leaf // (NZ * NC)
    z = (leaf // NC) % NZ
    c = leaf % NC
    d = 1 - 2 * c

    def dev(xx, zz, cc):
        return {"leaf": leaf_id(xx % NX, zz % NZ, cc), "rhs": y}

    def peer(k):
        return {"leaf": leaf, "rhs": (y + k) % NY}

    def remote(src, dst, ssem, rsem, who):
        return pltpu.make_async_remote_copy(
            src_ref=src, dst_ref=dst, send_sem=ssem, recv_sem=rsem,
            device_id=who, device_id_type=MESH,
        )

    def arrived(ref, sem):
        pltpu.make_async_copy(ref, ref, sem).wait()

    loads = [
        pltpu.make_async_copy(x_hbm, xb, in_sem.at[0]),
        pltpu.make_async_copy(v_hbm, vb, in_sem.at[1]),
        pltpu.make_async_copy(t_hbm, tg.at[:, y], in_sem.at[2]),
        pltpu.make_async_copy(u_hbm, ub, in_sem.at[3]),
    ]
    for cp in loads:
        cp.start()

    barrier = pltpu.get_barrier_semaphore()
    peers = [dev(x + dx, z, (c + dc) % NC) for dx in range(NX) for dc in range(NC) if dx or dc]
    z4 = (z // 4) * 4
    z2 = z4 + (z - z4 + 2) % 4
    z1 = (z // 2) * 2 + (1 - z % 2)
    peers += [dev(x, z + 1, c), dev(x, z + NZ - 1, c), dev(x, z2, c)]
    peers += [peer(k) for k in range(1, NY)]
    for who in peers:
        pl.semaphore_signal(barrier, inc=1, device_id=who, device_id_type=MESH)

    step = 256
    below = lax.broadcasted_iota(jnp.int32, (step, step), 0)
    above = lax.broadcasted_iota(jnp.int32, (step, step), 1)
    tri = (below < above).astype(F32).astype(BF16)
    carry = jnp.zeros((NB, 1), F32)
    names = lax.broadcasted_iota(jnp.int32, (NB, step), 0)
    for i in range(ROWS // step):
        own = owner_ref[:, i * step : (i + 1) * step]
        hot = (names == own).astype(F32)
        before = jnp.dot(hot.astype(BF16), tri, preferred_element_type=F32) + carry
        rank = jnp.sum(before * hot, axis=0, keepdims=True)
        slot[:, i * step : (i + 1) * step] = own.astype(F32) * CAP + rank
        carry = carry + jnp.sum(hot, axis=1, keepdims=True)

    pl.semaphore_wait(barrier, len(peers))
    for cp in loads[:3]:
        cp.wait()
    nloads = [pltpu.make_async_copy(n_hbm.at[g], nb.at[g], n_sem.at[g]) for g in range(8)]
    for cp in nloads:
        cp.start()

    rel = lax.broadcasted_iota(jnp.int32, (CAP, 1), 0)
    ranks = ((y + NY - rel // Q) % NY) * Q + rel % Q

    def permute(i):
        slots = slot[...]
        hots = []
        for k in range(NG):
            xx, cc = (x + k // NC) % NX, (c + k % NC) % NC
            zz = (z + NZ - (1 - 2 * cc) * (i + 1)) % NZ
            want = (ranks + leaf_id(xx, zz, cc) * CAP).astype(F32)
            hots.append((slots == want).astype(F32).astype(BF16))
        xp = jnp.dot(jnp.concatenate(hots, axis=0), xb[...].reshape(ROWS, 256), preferred_element_type=F32).astype(BF16)
        quarter = jnp.concatenate([h[0:Q] for h in hots], axis=0)
        vp = jnp.dot(quarter, vb[...], preferred_element_type=F32).astype(BF16)
        rx[i, :, 0] = xp[0:CAP].reshape(NY, Q, 256)
        rv[i, 0, 0] = vp[0:Q]
        sx[i] = xp[CAP:].reshape(NG - 1, NY, Q, 256)
        sv[i] = vp[Q:].reshape(NG - 1, Q, 256)
        for k in range(1, NG):
            who = dev(x + k // NC, z, (c + k % NC) % NC)
            remote(sv.at[i, k - 1], rv.at[i, 0, k], vs_sem.at[i], vr_sem.at[i], who).start()
        for k in range(1, NG):
            who = dev(x + k // NC, z, (c + k % NC) % NC)
            remote(sx.at[i, k - 1], rx.at[i, :, k], xs_sem.at[i], xr_sem.at[i], who).start()

    def share(i):
        arrived(rv.at[i, 0, pl.ds(1, NG - 1)], vr_sem.at[i])
        for k in range(1, NY):
            remote(rv.at[i, 0], rv.at[i, k], ys_sem.at[i], yr_sem.at[i], peer(k)).start()

    def place(i):
        want = (lax.broadcasted_iota(jnp.int32, (8 * CAP, 1), 0) + i * (8 * CAP)).astype(F32)
        hot = (slot[...] == want).astype(F32).astype(BF16)
        up = jnp.dot(hot, ub[...], preferred_element_type=F32).astype(BF16)
        us[pl.ds(i * 8, 8)] = up.reshape(8, CAP, 256)

    def near(i):
        nloads[i].wait()
        total = jnp.zeros((256, 256), F32)
        for j in range(7):
            keep = jnp.minimum(jnp.maximum(count_ref[i] - j, 0), 1).astype(F32)
            term = jnp.dot(nb[i, j], xb[index_ref[i, j]], preferred_element_type=F32)
            total = total + term * keep
        acc[i * 256 : i * 256 + 256, :] = total

    def product(i):
        arrived(rx.at[i, :, pl.ds(1, NG - 1)], xr_sem.at[i])
        arrived(rv.at[i, pl.ds(1, NY - 1)], yr_sem.at[i])
        vs = rv[i].reshape(NG * CAP, 256)
        xs = rx[i].reshape(NG * CAP, 256)
        return lax.dot_general(vs, xs, (((0,), (0,)), ((), ())), preferred_element_type=F32)

    nxt = dev(x, z + NZ + d, c)

    def ring_copy(s, q):
        return remote(ring.at[s, q], ring.at[s + 1, q], rs_sem.at[s, q], rr_sem.at[s, q], nxt)

    def ring_first():
        p = product(0)
        for q in range(2):
            ring[0, q] = p[:, HALF * q : HALF * q + HALF]
            ring_copy(0, q).start()

    def ring_step(s):
        p = product(s)
        for q in range(2):
            ring_copy(s - 1, q).wait_recv()
            ring[s, q] = ring[s, q] + p[:, HALF * q : HALF * q + HALF]
            ring_copy(s, q).start()

    tcopies = [
        remote(tg.at[:, y], tg.at[:, y], ts_sem.at[k - 1], tr_sem.at[k - 1], peer(k)) for k in range(1, NY)
    ]
    for cp in tcopies:
        cp.start()
    permute(0)
    permute(1)
    loads[3].wait()
    permute(2)
    share(0)
    place(0)
    permute(3)
    share(1)
    ring_first()
    place(1)

    def step_on(i, carry):
        permute(i + 2)
        share(i)
        ring_step(i - 1)
        place(i)
        return carry

    lax.fori_loop(2, NZ - 2, step_on, 0)
    for i in (NZ - 2, NZ - 1):
        share(i)
        ring_step(i - 1)
        place(i)
    for i in range(ROWS // 128):
        row = jnp.broadcast_to(slot[:, i * 128 : (i + 1) * 128], (128, 128))
        scol[i * 128 : (i + 1) * 128, :] = jnp.transpose(row)
    for cp in tcopies:
        cp.wait_recv()

    mates = [dev(x, z, 1 - c), dev(x, z1, c), dev(x, z2, c)]

    def swap(l, q):
        return remote(lvl.at[l, q], part.at[l, q], bs_sem.at[l, q], br_sem.at[l, q], mates[l])

    last = product(NZ - 1)
    for q in range(2):
        ring_copy(NZ - 2, q).wait_recv()
        lvl[0, q] = (ring[NZ - 1, q] + last[:, HALF * q : HALF * q + HALF]).astype(BF16)
        swap(0, q).start()

    sent = []

    def go(cp):
        cp.start()
        sent.append(cp)

    def item(e, f):
        return leaf_id((x + SHIFT[f]) % NX, (z + 2 * NZ - d * e) % NZ, c)

    def zsend(h, e, f, to):
        b = item(e, f)
        n = ES.index(to)
        way = d if to > 0 else -d
        go(remote(cb.at[b, h], cb.at[b, h], zs_sem.at[h, f, n], zr_sem.at[h, f, n], dev(x, z + NZ + way, c)))

    def znext(h, e, f):
        if 0 <= e < 4:
            zsend(h, e, f, e + 1)
        if -3 < e <= 0:
            zsend(h, e, f, e - 1)

    def xsend(h, e):
        b, n = item(e, 0), ES.index(e)
        for w in range(2):
            who = dev(x + (1 if w == 0 else NX - 1), z, c)
            go(remote(cb.at[b, h], cb.at[b, h], hs_sem.at[h, n, w], hr_sem.at[h, n, w], who))

    def xnext(h, e, f):
        b, n, w = item(e, f), ES.index(e), f - 1
        piece = cb.at[b, h, pl.ds(HALF * w, HALF)]
        who = dev(x + (1 if w == 0 else NX - 1), z, c)
        go(remote(piece, piece, fs_sem.at[h, n, w], fr_sem.at[h, n, w], who))

    def take(h, e, f):
        b, n = item(e, f), ES.index(e)
        along_x = f > 0 and (h == 1 or e == 0)
        if along_x and f < 3:
            arrived(cb.at[b, h], hr_sem.at[h, n, f - 1])
        elif along_x:
            for w in range(2):
                arrived(cb.at[b, h, pl.ds(HALF * w, HALF)], fr_sem.at[h, n, w])
        elif e != 0:
            arrived(cb.at[b, h], zr_sem.at[h, f, n])
        if h == 1:
            if f == 0:
                znext(h, e, f)
                xsend(h, e)
            elif f < 3:
                xnext(h, e, f)
        else:
            if e == 0 and f == 0:
                xsend(h, e)
            if e == 0 and 0 < f < 3:
                xnext(h, e, f)
            znext(h, e, f)

    def cross(e, f):
        n = UNITS.index((e, f))
        b = item(e, f)
        go(remote(cb.at[b], cb.at[b], cs_sem.at[n], cr_sem.at[n], dev(x, z, 1 - c)))

    for l in range(3):
        t = tg[l].reshape(256, 512)
        for q in range(2):
            total = jnp.dot(t[:, 0:256], lvl[l, q], preferred_element_type=F32)
            for g in FILL[l][q]:
                near(g)
            arrived(part.at[l, q], br_sem.at[l, q])
            total = total + jnp.dot(t[:, 256:512], part[l, q], preferred_element_type=F32)
            if l < 2:
                lvl[l + 1, q] = total.astype(BF16)
                swap(l + 1, q).start()
            else:
                cb[leaf, q] = total.astype(BF16)
                take(q, 0, 0)
    cross(0, 0)

    lanes = lax.broadcasted_iota(jnp.int32, (1, HALF), 1)

    def quad(units):
        rows, wants = [], []
        for e, f in units:
            mirror = e if e in (0, 4) else -e
            n = UNITS.index((mirror, f))
            zz = (z + 2 * NZ - d * e) % NZ
            xx = (x + SHIFT[f]) % NX
            theirs = leaf_id(xx, zz, 1 - c)
            arrived(cb.at[theirs], cr_sem.at[n])
            b0 = leaf_id(xx, zz, 0)
            wants.append((lanes + b0 * CAP).astype(F32))
            for cc in range(2):
                coeff = jnp.concatenate([cb[b0 + cc, 0], cb[b0 + cc, 1]], axis=1)
                rows.append(jnp.dot(us[b0 + cc], coeff, preferred_element_type=F32).astype(BF16))
        far = jnp.concatenate(rows, axis=0)

        def back(i, carry):
            span = pl.ds(pl.multiple_of(i * 256, 256), 256)
            col = scol[span, :]
            hot = jnp.concatenate([(col == w).astype(F32).astype(BF16) for w in wants], axis=1)
            acc[span, :] = acc[span, :] + jnp.dot(hot, far, preferred_element_type=F32)
            return carry

        lax.fori_loop(0, ROWS // 256, back, 0)

    done = 0
    ready = 1
    for r in range(1, 7):
        for e, f in ROUNDS[r]:
            for h in range(2):
                take(h, e, f)
            cross(e, f)
        while done + 4 <= ready:
            quad(UNITS[done : done + 4])
            done += 4
        ready += len(ROUNDS[r])
    while done < len(UNITS):
        quad(UNITS[done : done + 4])
        done += 4
    out_ref[...] = acc[...].astype(BF16)

    for cp in sent:
        cp.wait_send()
    for cp in tcopies:
        cp.wait_send()
    for l in range(3):
        for q in range(2):
            swap(l, q).wait_send()
    for i in range(NZ):
        arrived(sx.at[i], xs_sem.at[i])
        arrived(sv.at[i], vs_sem.at[i])
        arrived(rv.at[i, pl.ds(1, NY - 1)], ys_sem.at[i])
    for s in range(NZ - 1):
        for q in range(2):
            ring_copy(s, q).wait_send()


def on_device(
    fields, owner, source_basis, field_basis, transfer, near_blocks, near_index, near_count
):
    vmem = pl.BlockSpec(memory_space=pltpu.VMEM)
    smem = pl.BlockSpec(memory_space=pltpu.SMEM)
    hbm = pl.BlockSpec(memory_space=pl.ANY)
    dma = pltpu.SemaphoreType.DMA
    return pl.pallas_call(
        whole_kernel,
        out_shape=jax.ShapeDtypeStruct((ROWS, 256), BF16),
        in_specs=[vmem, smem, smem, hbm, hbm, hbm, hbm, hbm],
        out_specs=vmem,
        scratch_shapes=[
            pltpu.VMEM((8, 256, 256), BF16),
            pltpu.VMEM((ROWS, 256), BF16),
            pltpu.VMEM((ROWS, 256), BF16),
            pltpu.VMEM((8, 7, 256, 256), BF16),
            pltpu.VMEM((1, ROWS), F32),
            pltpu.VMEM((ROWS, HALF), F32),
            pltpu.VMEM((NZ, NG - 1, NY, Q, 256), BF16),
            pltpu.VMEM((NZ, NG - 1, Q, 256), BF16),
            pltpu.VMEM((NZ, NY, NG, Q, 256), BF16),
            pltpu.VMEM((NZ, NY, NG, Q, 256), BF16),
            pltpu.VMEM((NB, CAP, 256), BF16),
            pltpu.VMEM((NZ, 2, 256, HALF), F32),
            pltpu.VMEM((3, 2, 256, HALF), BF16),
            pltpu.VMEM((3, 2, 256, HALF), BF16),
            pltpu.VMEM((3, NY, 64, 512), BF16),
            pltpu.VMEM((NB, 2, 256, HALF), BF16),
            pltpu.VMEM((ROWS, 256), F32),
            dma((4,)), dma((8,)),
            dma((NZ,)), dma((NZ,)), dma((NZ,)), dma((NZ,)), dma((NZ,)), dma((NZ,)),
            dma((NZ, 2)), dma((NZ, 2)), dma((3, 2)), dma((3, 2)), dma((3,)), dma((3,)),
            dma((2, 4, 8)), dma((2, 4, 8)),
            dma((2, 8, 2)), dma((2, 8, 2)),
            dma((2, 8, 2)), dma((2, 8, 2)),
            dma((32,)), dma((32,)),
        ],
        compiler_params=pltpu.CompilerParams(
            collective_id=0, has_side_effects=True, vmem_limit_bytes=63 * 1024 * 1024
        ),
    )(
        owner.reshape(1, -1), near_index, near_count, fields.reshape(8, 256, 256), source_basis, field_basis,
        transfer[0], near_blocks,
    )


def solution(mesh):
    in_specs = (
        P("leaf", "rhs"),
        P("leaf", None),
        P("leaf", None),
        P("leaf", None),
        P("leaf", None, "rhs", None),
        P("leaf", None, None, None),
        P("leaf", None),
        P("leaf"),
    )
    return jax.shard_map(
        on_device, mesh=mesh, in_specs=in_specs, out_specs=P("leaf", "rhs"), check_vma=False
    )
```

time: 412 us -> 114 us (0.28)
  waiting for transfers between devices: 255 us -> 0 us
  Pallas kernels: 0 us -> 112 us
  local copies, waits for them, and re-layouts: 57.9 us -> 2.26 us
  blocking collectives: 28.9 us -> 0 us
  matrix products: 25.4 us -> 0 us
  other arithmetic: 23.5 us -> 0 us
  between operations: 13.5 us -> 0.01 us
  starting transfers between devices: 7.18 us -> 0 us
    reduce_scatter x1 -> x0, waiting for transfers between devices: 190 us -> none  [on_device(): lax.psum_scatter(jnp.einsum('bck,bcn->bkn', v_three, x_three, preferred_e...]
    pallas_call x0 -> x1, Pallas kernels: none -> 112 us  [on_device(): pl.pallas_call(whole_kernel, out_shape=jax.ShapeDtypeStruct((ROWS, 256),...]
    all_gather x1 -> x0, waiting for transfers between devices: 65.2 us -> none  [on_device(): lax.all_gather(coefficients[None], 'leaf', axis=0, tiled=True)]
    scatter x3 -> x0, local copies, waits for them, and re-layouts: 32.5 us -> none  [the longest x2 21.6 us: on_device(): jnp.zeros((n_leaf * capacity, basis_width), jnp.bfloat16).at[slot_index]]
    all_gather x3 -> x0, blocking collectives: 28.9 us -> none  [on_device(): lax.all_gather(transfer[0, level_num], 'rhs', axis=0, tiled=True)]
    dot_general x6 -> x0, matrix products: 25.4 us -> none  [the longest x1 9.68 us: on_device(): jnp.einsum('bck,bcn->bkn', v_three, x_three, preferred_element_type=jnp.f...]
    another operation x3 -> x0, other arithmetic: 18.5 us -> none
    gather x2 -> x0, local copies, waits for them, and re-layouts: 12.8 us -> none  [the longest x1 7.5 us: on_device(): far_term = far_slots[slot_index]]
  transfers between devices with their start and end apart: 5 -> 0, of which waited for: 2 -> 0; matrix products, arithmetic and copies ran while one was open for 6% -> 0% of each run, Pallas kernels for 0% -> 0%
where the time goes in v2:
time: 114 us
  Pallas kernels  112 us (98%)
  local copies, waits for them, and re-layouts  2.26 us (2%)
    pallas_call x1, Pallas kernels, on_device(): pl.pallas_call(whole_kernel, out_shape=jax.ShapeDtypeStruct((ROWS, 256),...  112 us

profile of v2, /device:TPU:1, one launch (start us, length us, event | category | flops | bytes accessed | tf_op | source)
XLA Modules:
  0.0 114.2 jit_solution(13847605850744931208)
XLA Ops:
  0.0 111.9 %shard_map.82 = bf16[2048,256]{1,0:T(8,128)(2,1)} custom-call(s32[1,2048]{1,0:T(1,128)} %bitcast.5, s32[8,7]{1,0:T(8,128)} %index_ref.1, s32[8]{0:T(128)} %count_ref.1, bf16[8,256,256]{2,1,0:T(8,128)(2,1)} %bitcast.3, bf16[2048,256]{1,0:T(8,128)(2,1)} %v_hbm.1, bf16[2048,256]{1,0:T(8,128)(2,1)} %u_hbm.1, bf16[3,64,512]{2,1,0:T(8,128)(2,1)} %bitcast.4, ...), custom_call_target="tpu_custom_call" | custom-call | tf_op jit(solution)/shard_map/pallas_call | solution.py:357
  112.0 2.3 %copy.10 = bf16[2048,256]{1,0:T(8,128)(2,1)} copy(bf16[2048,256]{1,0:T(8,128)(2,1)} %shard_map.82) | data formatting | bytes 2097152

commit v3 on v2

--- a/solution.py
+++ b/solution.py
@@ -20,7 +20,13 @@
 SHIFT = [0, NX - 1, 1, 2]
 ROUNDS = [[(e, f) for e in ES for f in range(4) if abs(e) + DIST[f] == r] for r in range(7)]
 UNITS = [u for r in ROUNDS for u in r]
-FILL = [[[0], []], [[1, 2], []], [[3, 4, 5, 6], [7]]]
+LATE = [3, -3, 4]
+ZSET = [(1, 0, n) for n in range(1, 8)]
+ZSET += [(0, f, n) for f in range(4) for n in range(1, 8) if f < 3 or ES[n] not in LATE]
+XSET = [(1, n, w) for n in range(8) for w in range(2)] + [(0, 0, 0), (0, 0, 1)]
+FSET = [(1, n) for n in range(8)] + [(0, 0)] + [(0, ES.index(e)) for e in LATE]
+SENT = (len(ZSET) + len(XSET) + len(FSET)) // 2 + len(UNITS)
+FILL = [[[], []], [[3, 4], []], [[5, 6, 7], []]]
 
 
 def leaf_id(x, z, c):
@@ -32,7 +38,7 @@
     xb, vb, ub, nb, slot, scol, sx, sv, rx, rv, us, ring, lvl, part, tg, cb, acc,
     in_sem, n_sem,
     xs_sem, xr_sem, vs_sem, vr_sem, ys_sem, yr_sem, rs_sem, rr_sem, bs_sem, br_sem, ts_sem, tr_sem,
-    zs_sem, zr_sem, hs_sem, hr_sem, fs_sem, fr_sem, cs_sem, cr_sem,
+    as_sem, zr_sem, hr_sem, fr_sem, cr_sem,
 ):
     leaf = lax.axis_index("leaf")
     y = lax.axis_index("rhs")
@@ -92,9 +98,8 @@
     pl.semaphore_wait(barrier, len(peers))
     for cp in loads[:3]:
         cp.wait()
-    nloads = [pltpu.make_async_copy(n_hbm.at[g], nb.at[g], n_sem.at[g]) for g in range(8)]
-    for cp in nloads:
-        cp.start()
+    nload = pltpu.make_async_copy(n_hbm, nb, n_sem)
+    nload.start()
 
     rel = lax.broadcasted_iota(jnp.int32, (CAP, 1), 0)
     ranks = ((y + NY - rel // Q) % NY) * Q + rel % Q
@@ -107,24 +112,24 @@
             zz = (z + NZ - (1 - 2 * cc) * (i + 1)) % NZ
             want = (ranks + leaf_id(xx, zz, cc) * CAP).astype(F32)
             hots.append((slots == want).astype(F32).astype(BF16))
-        xp = jnp.dot(jnp.concatenate(hots, axis=0), xb[...].reshape(ROWS, 256), preferred_element_type=F32).astype(BF16)
         quarter = jnp.concatenate([h[0:Q] for h in hots], axis=0)
         vp = jnp.dot(quarter, vb[...], preferred_element_type=F32).astype(BF16)
-        rx[i, :, 0] = xp[0:CAP].reshape(NY, Q, 256)
         rv[i, 0, 0] = vp[0:Q]
-        sx[i] = xp[CAP:].reshape(NG - 1, NY, Q, 256)
         sv[i] = vp[Q:].reshape(NG - 1, Q, 256)
         for k in range(1, NG):
             who = dev(x + k // NC, z, (c + k % NC) % NC)
-            remote(sv.at[i, k - 1], rv.at[i, 0, k], vs_sem.at[i], vr_sem.at[i], who).start()
+            remote(sv.at[i, k - 1], rv.at[i, 0, k], vs_sem, vr_sem.at[i], who).start()
+        xp = jnp.dot(jnp.concatenate(hots, axis=0), xb[...].reshape(ROWS, 256), preferred_element_type=F32).astype(BF16)
+        rx[i, :, 0] = xp[0:CAP].reshape(NY, Q, 256)
+        sx[i] = xp[CAP:].reshape(NG - 1, NY, Q, 256)
         for k in range(1, NG):
             who = dev(x + k // NC, z, (c + k % NC) % NC)
-            remote(sx.at[i, k - 1], rx.at[i, :, k], xs_sem.at[i], xr_sem.at[i], who).start()
+            remote(sx.at[i, k - 1], rx.at[i, :, k], xs_sem, xr_sem.at[i], who).start()
 
     def share(i):
         arrived(rv.at[i, 0, pl.ds(1, NG - 1)], vr_sem.at[i])
         for k in range(1, NY):
-            remote(rv.at[i, 0], rv.at[i, k], ys_sem.at[i], yr_sem.at[i], peer(k)).start()
+            remote(rv.at[i, 0], rv.at[i, k], ys_sem, yr_sem.at[i], peer(k)).start()
 
     def place(i):
         want = (lax.broadcasted_iota(jnp.int32, (8 * CAP, 1), 0) + i * (8 * CAP)).astype(F32)
@@ -133,7 +138,6 @@
         us[pl.ds(i * 8, 8)] = up.reshape(8, CAP, 256)
 
     def near(i):
-        nloads[i].wait()
         total = jnp.zeros((256, 256), F32)
         for j in range(7):
             keep = jnp.minimum(jnp.maximum(count_ref[i] - j, 0), 1).astype(F32)
@@ -151,7 +155,7 @@
     nxt = dev(x, z + NZ + d, c)
 
     def ring_copy(s, q):
-        return remote(ring.at[s, q], ring.at[s + 1, q], rs_sem.at[s, q], rr_sem.at[s, q], nxt)
+        return remote(ring.at[s, q], ring.at[s + 1, q], rs_sem, rr_sem.at[s, q], nxt)
 
     def ring_first():
         p = product(0)
@@ -159,51 +163,47 @@
             ring[0, q] = p[:, HALF * q : HALF * q + HALF]
             ring_copy(0, q).start()
 
-    def ring_step(s):
+    def ring_step(s, between):
         p = product(s)
         for q in range(2):
             ring_copy(s - 1, q).wait_recv()
             ring[s, q] = ring[s, q] + p[:, HALF * q : HALF * q + HALF]
             ring_copy(s, q).start()
-
-    tcopies = [
-        remote(tg.at[:, y], tg.at[:, y], ts_sem.at[k - 1], tr_sem.at[k - 1], peer(k)) for k in range(1, NY)
-    ]
-    for cp in tcopies:
-        cp.start()
+            if q == 0:
+                between()
+
+    def tsend(l):
+        for k in range(1, NY):
+            remote(tg.at[l, y], tg.at[l, y], ts_sem, tr_sem.at[l], peer(k)).start()
+
+    tsend(0)
     permute(0)
     permute(1)
+    share(0)
     loads[3].wait()
     permute(2)
-    share(0)
     place(0)
-    permute(3)
     share(1)
     ring_first()
-    place(1)
-
-    def step_on(i, carry):
-        permute(i + 2)
-        share(i)
-        ring_step(i - 1)
-        place(i)
+    permute(3)
+    share(2)
+
+    def step_on(m, carry):
+        ring_step(m - 2, lambda: permute(m + 1))
+        share(m)
         return carry
 
-    lax.fori_loop(2, NZ - 2, step_on, 0)
-    for i in (NZ - 2, NZ - 1):
-        share(i)
-        ring_step(i - 1)
-        place(i)
-    for i in range(ROWS // 128):
-        row = jnp.broadcast_to(slot[:, i * 128 : (i + 1) * 128], (128, 128))
-        scol[i * 128 : (i + 1) * 128, :] = jnp.transpose(row)
-    for cp in tcopies:
-        cp.wait_recv()
+    lax.fori_loop(3, NZ - 1, step_on, 0)
+    ring_step(NZ - 3, lambda: place(1))
+    share(NZ - 1)
+    tsend(1)
+    tsend(2)
+    ring_step(NZ - 2, lambda: place(2))
 
     mates = [dev(x, z, 1 - c), dev(x, z1, c), dev(x, z2, c)]
 
     def swap(l, q):
-        return remote(lvl.at[l, q], part.at[l, q], bs_sem.at[l, q], br_sem.at[l, q], mates[l])
+        return remote(lvl.at[l, q], part.at[l, q], bs_sem, br_sem.at[l, q], mates[l])
 
     last = product(NZ - 1)
     for q in range(2):
@@ -211,11 +211,8 @@
         lvl[0, q] = (ring[NZ - 1, q] + last[:, HALF * q : HALF * q + HALF]).astype(BF16)
         swap(0, q).start()
 
-    sent = []
-
     def go(cp):
         cp.start()
-        sent.append(cp)
 
     def item(e, f):
         return leaf_id((x + SHIFT[f]) % NX, (z + 2 * NZ - d * e) % NZ, c)
@@ -224,36 +221,36 @@
         b = item(e, f)
         n = ES.index(to)
         way = d if to > 0 else -d
-        go(remote(cb.at[b, h], cb.at[b, h], zs_sem.at[h, f, n], zr_sem.at[h, f, n], dev(x, z + NZ + way, c)))
+        go(remote(cb.at[b, h], cb.at[b, h], as_sem, zr_sem.at[ZSET.index((h, f, n))], dev(x, z + NZ + way, c)))
 
     def znext(h, e, f):
-        if 0 <= e < 4:
+        far_off = 2 if f == 3 else 4
+        if 0 <= e < far_off:
             zsend(h, e, f, e + 1)
-        if -3 < e <= 0:
+        if -min(far_off, 3) < e <= 0:
             zsend(h, e, f, e - 1)
 
     def xsend(h, e):
         b, n = item(e, 0), ES.index(e)
         for w in range(2):
             who = dev(x + (1 if w == 0 else NX - 1), z, c)
-            go(remote(cb.at[b, h], cb.at[b, h], hs_sem.at[h, n, w], hr_sem.at[h, n, w], who))
+            go(remote(cb.at[b, h], cb.at[b, h], as_sem, hr_sem.at[XSET.index((h, n, w))], who))
 
     def xnext(h, e, f):
         b, n, w = item(e, f), ES.index(e), f - 1
         piece = cb.at[b, h, pl.ds(HALF * w, HALF)]
         who = dev(x + (1 if w == 0 else NX - 1), z, c)
-        go(remote(piece, piece, fs_sem.at[h, n, w], fr_sem.at[h, n, w], who))
+        go(remote(piece, piece, as_sem, fr_sem.at[FSET.index((h, n))], who))
 
     def take(h, e, f):
         b, n = item(e, f), ES.index(e)
-        along_x = f > 0 and (h == 1 or e == 0)
+        along_x = f > 0 and (h == 1 or e == 0 or (f == 3 and e in LATE))
         if along_x and f < 3:
-            arrived(cb.at[b, h], hr_sem.at[h, n, f - 1])
+            arrived(cb.at[b, h], hr_sem.at[XSET.index((h, n, f - 1))])
         elif along_x:
-            for w in range(2):
-                arrived(cb.at[b, h, pl.ds(HALF * w, HALF)], fr_sem.at[h, n, w])
+            arrived(cb.at[b, h], fr_sem.at[FSET.index((h, n))])
         elif e != 0:
-            arrived(cb.at[b, h], zr_sem.at[h, f, n])
+            arrived(cb.at[b, h], zr_sem.at[ZSET.index((h, f, n))])
         if h == 1:
             if f == 0:
                 znext(h, e, f)
@@ -263,21 +260,29 @@
         else:
             if e == 0 and f == 0:
                 xsend(h, e)
-            if e == 0 and 0 < f < 3:
+            if (e == 0 or e in LATE) and 0 < f < 3:
                 xnext(h, e, f)
             znext(h, e, f)
 
     def cross(e, f):
         n = UNITS.index((e, f))
         b = item(e, f)
-        go(remote(cb.at[b], cb.at[b], cs_sem.at[n], cr_sem.at[n], dev(x, z, 1 - c)))
+        go(remote(cb.at[b], cb.at[b], as_sem, cr_sem.at[n], dev(x, z, 1 - c)))
+
+    def columns():
+        for i in range(ROWS // 128):
+            row = jnp.broadcast_to(slot[:, i * 128 : (i + 1) * 128], (128, 128))
+            scol[i * 128 : (i + 1) * 128, :] = jnp.transpose(row).astype(jnp.int32).astype(jnp.int16)
 
     for l in range(3):
+        arrived(tg.at[l, pl.ds(0, NY - 1)], tr_sem.at[l])
         t = tg[l].reshape(256, 512)
         for q in range(2):
             total = jnp.dot(t[:, 0:256], lvl[l, q], preferred_element_type=F32)
+            if (l, q) == (0, 0):
+                columns()
             for g in FILL[l][q]:
-                near(g)
+                place(g)
             arrived(part.at[l, q], br_sem.at[l, q])
             total = total + jnp.dot(t[:, 256:512], part[l, q], preferred_element_type=F32)
             if l < 2:
@@ -287,8 +292,12 @@
                 cb[leaf, q] = total.astype(BF16)
                 take(q, 0, 0)
     cross(0, 0)
-
-    lanes = lax.broadcasted_iota(jnp.int32, (1, HALF), 1)
+    nload.wait()
+    for g in range(6):
+        near(g)
+
+    lanes = lax.broadcasted_iota(jnp.int32, (16, HALF), 1)
+    one, zero = jnp.ones((), BF16), jnp.zeros((), BF16)
 
     def quad(units):
         rows, wants = [], []
@@ -300,20 +309,15 @@
             theirs = leaf_id(xx, zz, 1 - c)
             arrived(cb.at[theirs], cr_sem.at[n])
             b0 = leaf_id(xx, zz, 0)
-            wants.append((lanes + b0 * CAP).astype(F32))
+            wants.append((lanes + b0 * CAP).astype(jnp.int16)[None])
             for cc in range(2):
                 coeff = jnp.concatenate([cb[b0 + cc, 0], cb[b0 + cc, 1]], axis=1)
                 rows.append(jnp.dot(us[b0 + cc], coeff, preferred_element_type=F32).astype(BF16))
         far = jnp.concatenate(rows, axis=0)
 
-        def back(i, carry):
-            span = pl.ds(pl.multiple_of(i * 256, 256), 256)
-            col = scol[span, :]
-            hot = jnp.concatenate([(col == w).astype(F32).astype(BF16) for w in wants], axis=1)
-            acc[span, :] = acc[span, :] + jnp.dot(hot, far, preferred_element_type=F32)
-            return carry
-
-        lax.fori_loop(0, ROWS // 256, back, 0)
+        col = scol[...].reshape(ROWS // 16, 16, HALF)
+        hot = jnp.concatenate([jnp.where(col == w, one, zero).reshape(ROWS, HALF) for w in wants], axis=1)
+        acc[...] = acc[...] + jnp.dot(hot, far, preferred_element_type=F32)
 
     done = 0
     ready = 1
@@ -322,6 +326,9 @@
             for h in range(2):
                 take(h, e, f)
             cross(e, f)
+        if r == 1:
+            near(6)
+            near(7)
         while done + 4 <= ready:
             quad(UNITS[done : done + 4])
             done += 4
@@ -331,20 +338,13 @@
         done += 4
     out_ref[...] = acc[...].astype(BF16)
 
-    for cp in sent:
-        cp.wait_send()
-    for cp in tcopies:
-        cp.wait_send()
-    for l in range(3):
-        for q in range(2):
-            swap(l, q).wait_send()
-    for i in range(NZ):
-        arrived(sx.at[i], xs_sem.at[i])
-        arrived(sv.at[i], vs_sem.at[i])
-        arrived(rv.at[i, pl.ds(1, NY - 1)], ys_sem.at[i])
-    for s in range(NZ - 1):
-        for q in range(2):
-            ring_copy(s, q).wait_send()
+    arrived(cb.at[pl.ds(0, SENT)], as_sem)
+    arrived(tg.at[:, pl.ds(0, NY - 1)], ts_sem)
+    arrived(lvl, bs_sem)
+    arrived(sx, xs_sem)
+    arrived(sv, vs_sem)
+    arrived(rv.at[:, pl.ds(1, NY - 1)], ys_sem)
+    arrived(ring.at[pl.ds(0, NZ - 1)], rs_sem)
 
 
 def on_device(
@@ -365,7 +365,7 @@
             pltpu.VMEM((ROWS, 256), BF16),
             pltpu.VMEM((8, 7, 256, 256), BF16),
             pltpu.VMEM((1, ROWS), F32),
-            pltpu.VMEM((ROWS, HALF), F32),
+            pltpu.VMEM((ROWS, HALF), jnp.int16),
             pltpu.VMEM((NZ, NG - 1, NY, Q, 256), BF16),
             pltpu.VMEM((NZ, NG - 1, Q, 256), BF16),
             pltpu.VMEM((NZ, NY, NG, Q, 256), BF16),
@@ -377,13 +377,10 @@
             pltpu.VMEM((3, NY, 64, 512), BF16),
             pltpu.VMEM((NB, 2, 256, HALF), BF16),
             pltpu.VMEM((ROWS, 256), F32),
-            dma((4,)), dma((8,)),
-            dma((NZ,)), dma((NZ,)), dma((NZ,)), dma((NZ,)), dma((NZ,)), dma((NZ,)),
-            dma((NZ, 2)), dma((NZ, 2)), dma((3, 2)), dma((3, 2)), dma((3,)), dma((3,)),
-            dma((2, 4, 8)), dma((2, 4, 8)),
-            dma((2, 8, 2)), dma((2, 8, 2)),
-            dma((2, 8, 2)), dma((2, 8, 2)),
-            dma((32,)), dma((32,)),
+            dma((4,)), dma(()),
+            dma(()), dma((NZ,)), dma(()), dma((NZ,)), dma(()), dma((NZ,)),
+            dma(()), dma((NZ, 2)), dma(()), dma((3, 2)), dma(()), dma((3,)),
+            dma(()), dma((len(ZSET),)), dma((len(XSET),)), dma((len(FSET),)), dma((len(UNITS),)),
         ],
         compiler_params=pltpu.CompilerParams(
             collective_id=0, has_side_effects=True, vmem_limit_bytes=63 * 1024 * 1024

time: 114 us -> 104 us (0.912)
  Pallas kernels: 112 us -> 101 us
    pallas_call x1, Pallas kernels: 112 us -> 101 us  [on_device(): pl.pallas_call(whole_kernel, out_shape=jax.ShapeDtypeStruct((ROWS, 256),...]
where the time goes in v3:
time: 104 us; the launch traced here: 103 us
  Pallas kernels  101 us (97%)
  local copies, waits for them, and re-layouts  2.26 us (2%)
    pallas_call x1, Pallas kernels, on_device(): pl.pallas_call(whole_kernel, out_shape=jax.ShapeDtypeStruct((ROWS, 256),...  101 us
    unnamed x1, local copies, waits for them, and re-layouts  2.26 us

profile of v3, /device:TPU:1, one launch (start us, length us, event | category | flops | bytes accessed | tf_op | source)
XLA Modules:
  0.0 103.4 jit_solution(3065943338138232240)
XLA Ops:
  0.0 101.1 %shard_map.82 = bf16[2048,256]{1,0:T(8,128)(2,1)} custom-call(s32[1,2048]{1,0:T(1,128)} %bitcast.5, s32[8,7]{1,0:T(8,128)} %index_ref.1, s32[8]{0:T(128)} %count_ref.1, bf16[8,256,256]{2,1,0:T(8,128)(2,1)} %bitcast.3, bf16[2048,256]{1,0:T(8,128)(2,1)} %v_hbm.1, bf16[2048,256]{1,0:T(8,128)(2,1)} %u_hbm.1, bf16[3,64,512]{2,1,0:T(8,128)(2,1)} %bitcast.4, ...), custom_call_target="tpu_custom_call" | custom-call | tf_op jit(solution)/shard_map/pallas_call | solution.py:357
  101.1 2.3 %copy.10 = bf16[2048,256]{1,0:T(8,128)(2,1)} copy(bf16[2048,256]{1,0:T(8,128)(2,1)} %shard_map.82) | data formatting | bytes 2097152

commit v4 on v3

--- a/solution.py
+++ b/solution.py
@@ -15,12 +15,15 @@
 Q = CAP // NY
 ROWS = 2048
 HALF = 128
+RING = F32
+PIECES = [(0, 0), (HALF, 0), (0, HALF), (HALF, HALF)]
 ES = [0, 1, -1, 2, -2, 3, -3, 4]
 DIST = [0, 1, 1, 2]
 SHIFT = [0, NX - 1, 1, 2]
 ROUNDS = [[(e, f) for e in ES for f in range(4) if abs(e) + DIST[f] == r] for r in range(7)]
 UNITS = [u for r in ROUNDS for u in r]
 LATE = [3, -3, 4]
+GROUPS = [[], [], [(0, 4)], [(4, 8), (8, 12)], [(12, 16), (16, 20)], [(20, 24), (24, 27)], [(27, 31), (31, 32)]]
 ZSET = [(1, 0, n) for n in range(1, 8)]
 ZSET += [(0, f, n) for f in range(4) for n in range(1, 8) if f < 3 or ES[n] not in LATE]
 XSET = [(1, n, w) for n in range(8) for w in range(2)] + [(0, 0, 0), (0, 0, 1)]
@@ -104,22 +107,26 @@
     rel = lax.broadcasted_iota(jnp.int32, (CAP, 1), 0)
     ranks = ((y + NY - rel // Q) % NY) * Q + rel % Q
 
-    def permute(i):
+    def hots(i, ranks):
         slots = slot[...]
-        hots = []
+        rows = []
         for k in range(NG):
             xx, cc = (x + k // NC) % NX, (c + k % NC) % NC
             zz = (z + NZ - (1 - 2 * cc) * (i + 1)) % NZ
             want = (ranks + leaf_id(xx, zz, cc) * CAP).astype(F32)
-            hots.append((slots == want).astype(F32).astype(BF16))
-        quarter = jnp.concatenate([h[0:Q] for h in hots], axis=0)
-        vp = jnp.dot(quarter, vb[...], preferred_element_type=F32).astype(BF16)
+            rows.append((slots == want).astype(F32).astype(BF16))
+        return jnp.concatenate(rows, axis=0)
+
+    def send_v(i):
+        vp = jnp.dot(hots(i, ranks[0:Q]), vb[...], preferred_element_type=F32).astype(BF16)
         rv[i, 0, 0] = vp[0:Q]
         sv[i] = vp[Q:].reshape(NG - 1, Q, 256)
         for k in range(1, NG):
             who = dev(x + k // NC, z, (c + k % NC) % NC)
             remote(sv.at[i, k - 1], rv.at[i, 0, k], vs_sem, vr_sem.at[i], who).start()
-        xp = jnp.dot(jnp.concatenate(hots, axis=0), xb[...].reshape(ROWS, 256), preferred_element_type=F32).astype(BF16)
+
+    def send_x(i):
+        xp = jnp.dot(hots(i, ranks), xb[...].reshape(ROWS, 256), preferred_element_type=F32).astype(BF16)
         rx[i, :, 0] = xp[0:CAP].reshape(NY, Q, 256)
         sx[i] = xp[CAP:].reshape(NG - 1, NY, Q, 256)
         for k in range(1, NG):
@@ -157,48 +164,68 @@
     def ring_copy(s, q):
         return remote(ring.at[s, q], ring.at[s + 1, q], rs_sem, rr_sem.at[s, q], nxt)
 
+    def piece(p, q):
+        k, n = PIECES[q]
+        return p[k : k + HALF, n : n + HALF]
+
     def ring_first():
         p = product(0)
-        for q in range(2):
-            ring[0, q] = p[:, HALF * q : HALF * q + HALF]
+        for q in range(4):
+            ring[0, q] = piece(p, q).astype(RING)
             ring_copy(0, q).start()
 
-    def ring_step(s, between):
+    def ring_step(s, first, second):
         p = product(s)
-        for q in range(2):
+        for q in range(4):
             ring_copy(s - 1, q).wait_recv()
-            ring[s, q] = ring[s, q] + p[:, HALF * q : HALF * q + HALF]
+            ring[s, q] = (ring[s, q].astype(F32) + piece(p, q)).astype(RING)
             ring_copy(s, q).start()
             if q == 0:
-                between()
+                first()
+            if q == 2:
+                second()
 
     def tsend(l):
         for k in range(1, NY):
             remote(tg.at[l, y], tg.at[l, y], ts_sem, tr_sem.at[l], peer(k)).start()
 
     tsend(0)
-    permute(0)
-    permute(1)
+    send_v(0)
+    send_x(0)
+    send_v(1)
     share(0)
+    send_x(1)
+    send_v(2)
     loads[3].wait()
-    permute(2)
     place(0)
     share(1)
+    send_x(2)
+    send_v(3)
     ring_first()
-    permute(3)
+    send_x(3)
     share(2)
+    send_v(4)
+    send_x(4)
+    send_v(5)
 
     def step_on(m, carry):
-        ring_step(m - 2, lambda: permute(m + 1))
         share(m)
+        ring_step(m - 2, lambda: send_v(m + 3), lambda: send_x(m + 2))
         return carry
 
-    lax.fori_loop(3, NZ - 1, step_on, 0)
-    ring_step(NZ - 3, lambda: place(1))
+    def rest():
+        return None
+
+    lax.fori_loop(3, NZ - 3, step_on, 0)
+    share(NZ - 3)
+    ring_step(NZ - 5, rest, lambda: send_x(NZ - 1))
+    share(NZ - 2)
+    ring_step(NZ - 4, rest, lambda: place(1))
     share(NZ - 1)
     tsend(1)
     tsend(2)
-    ring_step(NZ - 2, lambda: place(2))
+    ring_step(NZ - 3, rest, lambda: place(2))
+    ring_step(NZ - 2, rest, rest)
 
     mates = [dev(x, z, 1 - c), dev(x, z1, c), dev(x, z2, c)]
 
@@ -207,8 +234,10 @@
 
     last = product(NZ - 1)
     for q in range(2):
-        ring_copy(NZ - 2, q).wait_recv()
-        lvl[0, q] = (ring[NZ - 1, q] + last[:, HALF * q : HALF * q + HALF]).astype(BF16)
+        for h in range(2):
+            ring_copy(NZ - 2, 2 * q + h).wait_recv()
+            total = ring[NZ - 1, 2 * q + h].astype(F32) + piece(last, 2 * q + h)
+            lvl[0, q, HALF * h : HALF * h + HALF, :] = total.astype(BF16)
         swap(0, q).start()
 
     def go(cp):
@@ -315,12 +344,15 @@
                 rows.append(jnp.dot(us[b0 + cc], coeff, preferred_element_type=F32).astype(BF16))
         far = jnp.concatenate(rows, axis=0)
 
-        col = scol[...].reshape(ROWS // 16, 16, HALF)
-        hot = jnp.concatenate([jnp.where(col == w, one, zero).reshape(ROWS, HALF) for w in wants], axis=1)
-        acc[...] = acc[...] + jnp.dot(hot, far, preferred_element_type=F32)
-
-    done = 0
-    ready = 1
+        def back(i, carry):
+            span = pl.ds(pl.multiple_of(i * 1024, 1024), 1024)
+            col = scol[span, :].reshape(1024 // 16, 16, HALF)
+            hot = jnp.concatenate([jnp.where(col == w, one, zero).reshape(1024, HALF) for w in wants], axis=1)
+            acc[span, :] = acc[span, :] + jnp.dot(hot, far, preferred_element_type=F32)
+            return carry
+
+        lax.fori_loop(0, ROWS // 1024, back, 0)
+
     for r in range(1, 7):
         for e, f in ROUNDS[r]:
             for h in range(2):
@@ -329,13 +361,8 @@
         if r == 1:
             near(6)
             near(7)
-        while done + 4 <= ready:
-            quad(UNITS[done : done + 4])
-            done += 4
-        ready += len(ROUNDS[r])
-    while done < len(UNITS):
-        quad(UNITS[done : done + 4])
-        done += 4
+        for lo, hi in GROUPS[r]:
+            quad(UNITS[lo:hi])
     out_ref[...] = acc[...].astype(BF16)
 
     arrived(cb.at[pl.ds(0, SENT)], as_sem)
@@ -356,7 +383,7 @@
     dma = pltpu.SemaphoreType.DMA
     return pl.pallas_call(
         whole_kernel,
-        out_shape=jax.ShapeDtypeStruct((ROWS, 256), BF16),
+        out_shape=pltpu.VMEM((ROWS, 256), BF16),
         in_specs=[vmem, smem, smem, hbm, hbm, hbm, hbm, hbm],
         out_specs=vmem,
         scratch_shapes=[
@@ -371,7 +398,7 @@
             pltpu.VMEM((NZ, NY, NG, Q, 256), BF16),
             pltpu.VMEM((NZ, NY, NG, Q, 256), BF16),
             pltpu.VMEM((NB, CAP, 256), BF16),
-            pltpu.VMEM((NZ, 2, 256, HALF), F32),
+            pltpu.VMEM((NZ, 4, HALF, HALF), RING),
             pltpu.VMEM((3, 2, 256, HALF), BF16),
             pltpu.VMEM((3, 2, 256, HALF), BF16),
             pltpu.VMEM((3, NY, 64, 512), BF16),
@@ -379,11 +406,11 @@
             pltpu.VMEM((ROWS, 256), F32),
             dma((4,)), dma(()),
             dma(()), dma((NZ,)), dma(()), dma((NZ,)), dma(()), dma((NZ,)),
-            dma(()), dma((NZ, 2)), dma(()), dma((3, 2)), dma(()), dma((3,)),
+            dma(()), dma((NZ - 1, 4)), dma(()), dma((3, 2)), dma(()), dma((3,)),
             dma(()), dma((len(ZSET),)), dma((len(XSET),)), dma((len(FSET),)), dma((len(UNITS),)),
         ],
         compiler_params=pltpu.CompilerParams(
-            collective_id=0, has_side_effects=True, vmem_limit_bytes=63 * 1024 * 1024
+            collective_id=0, has_side_effects=True, vmem_limit_bytes=58 * 1024 * 1024
         ),
     )(
         owner.reshape(1, -1), near_index, near_count, fields.reshape(8, 256, 256), source_basis, field_basis,

time: 104 us -> 98.8 us (0.950)
  Pallas kernels: 101 us -> 97.7 us
  local copies, waits for them, and re-layouts: 2.26 us -> 0.97 us
    pallas_call x1, Pallas kernels: 101 us -> 97.7 us  [on_device(): pl.pallas_call(whole_kernel, out_shape=pltpu.VMEM((ROWS, 256), BF16), in_...]
    unnamed x1, local copies, waits for them, and re-layouts: 2.26 us -> 0.97 us
where the time goes in v4:
time: 98.8 us; the launch traced here: 98.7 us
  Pallas kernels  97.7 us (99%)
    pallas_call x1, Pallas kernels, on_device(): pl.pallas_call(whole_kernel, out_shape=pltpu.VMEM((ROWS, 256), BF16), in_...  97.7 us

profile of v4, /device:TPU:1, one launch (start us, length us, event | category | flops | bytes accessed | tf_op | source)
XLA Modules:
  0.0 98.7 jit_solution(8318325778793464569)
XLA Ops:
  0.0 97.7 %shard_map.82 = bf16[2048,256]{1,0:T(8,128)(2,1)S(1)} custom-call(s32[1,2048]{1,0:T(1,128)} %bitcast.5, s32[8,7]{1,0:T(8,128)} %index_ref.1, s32[8]{0:T(128)} %count_ref.1, bf16[8,256,256]{2,1,0:T(8,128)(2,1)} %bitcast.3, bf16[2048,256]{1,0:T(8,128)(2,1)} %v_hbm.1, bf16[2048,256]{1,0:T(8,128)(2,1)} %u_hbm.1, bf16[3,64,512]{2,1,0:T(8,128)(2,1)} %bitcast.4, ...), custom_call_target="tpu_custom_call" | custom-call | tf_op jit(solution)/shard_map/pallas_call | solution.py:384
  97.7 1.0 copy.10

commit v5 on v4

--- a/solution.py
+++ b/solution.py
@@ -23,7 +23,8 @@
 ROUNDS = [[(e, f) for e in ES for f in range(4) if abs(e) + DIST[f] == r] for r in range(7)]
 UNITS = [u for r in ROUNDS for u in r]
 LATE = [3, -3, 4]
-GROUPS = [[], [], [(0, 4)], [(4, 8), (8, 12)], [(12, 16), (16, 20)], [(20, 24), (24, 27)], [(27, 31), (31, 32)]]
+GROUPS = {11: [(0, 4), (4, 8)], 19: [(8, 12), (12, 16)], 26: [(16, 20), (20, 24)]}
+GROUPS.update({30: [(24, 27)], 31: [(27, 31), (31, 32)]})
 ZSET = [(1, 0, n) for n in range(1, 8)]
 ZSET += [(0, f, n) for f in range(4) for n in range(1, 8) if f < 3 or ES[n] not in LATE]
 XSET = [(1, n, w) for n in range(8) for w in range(2)] + [(0, 0, 0), (0, 0, 1)]
@@ -353,15 +354,18 @@
 
         lax.fori_loop(0, ROWS // 1024, back, 0)
 
+    n = 1
     for r in range(1, 7):
         for e, f in ROUNDS[r]:
-            for h in range(2):
-                take(h, e, f)
+            take(0, e, f)
+        for e, f in ROUNDS[r]:
+            take(1, e, f)
             cross(e, f)
+        n += len(ROUNDS[r])
         if r == 1:
             near(6)
             near(7)
-        for lo, hi in GROUPS[r]:
+        for lo, hi in GROUPS.get(n - 1, []):
             quad(UNITS[lo:hi])
     out_ref[...] = acc[...].astype(BF16)
 

time: 98.8 us -> 96.8 us (0.980)
  Pallas kernels: 97.7 us -> 95.7 us
    pallas_call x1, Pallas kernels: 97.7 us -> 95.7 us  [on_device(): pl.pallas_call(whole_kernel, out_shape=pltpu.VMEM((ROWS, 256), BF16), in_...]
where the time goes in v5:
time: 96.8 us; the launch traced here: 96.6 us
  Pallas kernels  95.7 us (99%)
  local copies, waits for them, and re-layouts  0.97 us (1%)
    pallas_call x1, Pallas kernels, on_device(): pl.pallas_call(whole_kernel, out_shape=pltpu.VMEM((ROWS, 256), BF16), in_...  95.7 us

profile of v5, /device:TPU:1, one launch (start us, length us, event | category | flops | bytes accessed | tf_op | source)
XLA Modules:
  0.0 96.6 jit_solution(11281730202293958890)
XLA Ops:
  0.0 95.7 %shard_map.82 = bf16[2048,256]{1,0:T(8,128)(2,1)S(1)} custom-call(s32[1,2048]{1,0:T(1,128)} %bitcast.5, s32[8,7]{1,0:T(8,128)} %index_ref.1, s32[8]{0:T(128)} %count_ref.1, bf16[8,256,256]{2,1,0:T(8,128)(2,1)} %bitcast.3, bf16[2048,256]{1,0:T(8,128)(2,1)} %v_hbm.1, bf16[2048,256]{1,0:T(8,128)(2,1)} %u_hbm.1, bf16[3,64,512]{2,1,0:T(8,128)(2,1)} %bitcast.4, ...), custom_call_target="tpu_custom_call" | custom-call | tf_op jit(solution)/shard_map/pallas_call | solution.py:388
  95.7 1.0 %copy.10 = bf16[2048,256]{1,0:T(8,128)(2,1)} copy(bf16[2048,256]{1,0:T(8,128)(2,1)S(1)} %shard_map.82) | data formatting | bytes 2097152

commit v6 on v5

--- a/solution.py
+++ b/solution.py
@@ -15,7 +15,7 @@
 Q = CAP // NY
 ROWS = 2048
 HALF = 128
-RING = F32
+RING = BF16
 PIECES = [(0, 0), (HALF, 0), (0, HALF), (HALF, HALF)]
 ES = [0, 1, -1, 2, -2, 3, -3, 4]
 DIST = [0, 1, 1, 2]

time: 96.8 us -> 94.2 us (0.973)
  Pallas kernels: 95.7 us -> 93.1 us
    pallas_call x1, Pallas kernels: 95.7 us -> 93.1 us  [on_device(): pl.pallas_call(whole_kernel, out_shape=pltpu.VMEM((ROWS, 256), BF16), in_...]
where the time goes in v6:
time: 94.2 us; the launch traced here: 94.1 us
  Pallas kernels  93.1 us (99%)
  local copies, waits for them, and re-layouts  0.97 us (1%)
    pallas_call x1, Pallas kernels, on_device(): pl.pallas_call(whole_kernel, out_shape=pltpu.VMEM((ROWS, 256), BF16), in_...  93.1 us

profile of v6, /device:TPU:1, one launch (start us, length us, event | category | flops | bytes accessed | tf_op | source)
XLA Modules:
  0.0 94.1 jit_solution(12700496887376978088)
XLA Ops:
  0.0 93.1 %shard_map.82 = bf16[2048,256]{1,0:T(8,128)(2,1)S(1)} custom-call(s32[1,2048]{1,0:T(1,128)} %bitcast.5, s32[8,7]{1,0:T(8,128)} %index_ref.1, s32[8]{0:T(128)} %count_ref.1, bf16[8,256,256]{2,1,0:T(8,128)(2,1)} %bitcast.3, bf16[2048,256]{1,0:T(8,128)(2,1)} %v_hbm.1, bf16[2048,256]{1,0:T(8,128)(2,1)} %u_hbm.1, bf16[3,64,512]{2,1,0:T(8,128)(2,1)} %bitcast.4, ...), custom_call_target="tpu_custom_call" | custom-call | tf_op jit(solution)/shard_map/pallas_call | solution.py:388
  93.1 1.0 %copy.10 = bf16[2048,256]{1,0:T(8,128)(2,1)} copy(bf16[2048,256]{1,0:T(8,128)(2,1)S(1)} %shard_map.82) | data formatting | bytes 2097152

commit v7 on v5

--- a/solution.py
+++ b/solution.py
@@ -30,7 +30,7 @@
 XSET = [(1, n, w) for n in range(8) for w in range(2)] + [(0, 0, 0), (0, 0, 1)]
 FSET = [(1, n) for n in range(8)] + [(0, 0)] + [(0, ES.index(e)) for e in LATE]
 SENT = (len(ZSET) + len(XSET) + len(FSET)) // 2 + len(UNITS)
-FILL = [[[], []], [[3, 4], []], [[5, 6, 7], []]]
+FILL = [[[], []], [[1, 2, 3], []], [[4, 5, 6, 7], []]]
 
 
 def leaf_id(x, z, c):
@@ -221,11 +221,11 @@
     share(NZ - 3)
     ring_step(NZ - 5, rest, lambda: send_x(NZ - 1))
     share(NZ - 2)
-    ring_step(NZ - 4, rest, lambda: place(1))
+    ring_step(NZ - 4, rest, rest)
     share(NZ - 1)
     tsend(1)
     tsend(2)
-    ring_step(NZ - 3, rest, lambda: place(2))
+    ring_step(NZ - 3, rest, rest)
     ring_step(NZ - 2, rest, rest)
 
     mates = [dev(x, z, 1 - c), dev(x, z1, c), dev(x, z2, c)]

time: 96.8 us -> 96.7 us (level)
  no operation moved by 1% of the time
where the time goes in v7:
time: 96.7 us; the launch traced here: 96.6 us
  Pallas kernels  95.6 us (99%)
  local copies, waits for them, and re-layouts  0.97 us (1%)
    pallas_call x1, Pallas kernels, on_device(): pl.pallas_call(whole_kernel, out_shape=pltpu.VMEM((ROWS, 256), BF16), in_...  95.6 us

profile of v7, /device:TPU:1, one launch (start us, length us, event | category | flops | bytes accessed | tf_op | source)
XLA Modules:
  0.0 96.6 jit_solution(21718199899609459)
XLA Ops:
  0.0 95.6 %shard_map.82 = bf16[2048,256]{1,0:T(8,128)(2,1)S(1)} custom-call(s32[1,2048]{1,0:T(1,128)} %bitcast.5, s32[8,7]{1,0:T(8,128)} %index_ref.1, s32[8]{0:T(128)} %count_ref.1, bf16[8,256,256]{2,1,0:T(8,128)(2,1)} %bitcast.3, bf16[2048,256]{1,0:T(8,128)(2,1)} %v_hbm.1, bf16[2048,256]{1,0:T(8,128)(2,1)} %u_hbm.1, bf16[3,64,512]{2,1,0:T(8,128)(2,1)} %bitcast.4, ...), custom_call_target="tpu_custom_call" | custom-call | tf_op jit(solution)/shard_map/pallas_call | solution.py:388
  95.6 1.0 %copy.10 = bf16[2048,256]{1,0:T(8,128)(2,1)} copy(bf16[2048,256]{1,0:T(8,128)(2,1)S(1)} %shard_map.82) | data formatting | bytes 2097152
